TPU v7x, 32 devices: a whole 2x2x4 slice. The times are simulated.
32 devices in a mesh: section: 8 (over z, x), sp: 4 (over y, core).
Axes of the slice: x: 2, y: 2, z: 4, core: 2. Of those that a mesh axis runs over, the one named last changes fastest.
Arguments:
- slots: bfloat16 [8, 64, 3072], P('section', 'sp'), may hold values from -6 to 6
- patch_of_slot: int32 [8], replicated, may hold values from 0 to 7, each once
- step_of_slot: int32 [8], replicated, may hold values from 0 to 26
- modulation: bfloat16 [8, 28, 3, 3072], P('section'), may hold values from -4 to 4
- w_qkv: bfloat16 [8, 3072, 3, 2048], P('section', None, None, 'sp'), may hold values from -0.109375 to 0.109375
- qk_scale: bfloat16 [8, 2, 128], P('section'), may hold values from 0.25 to 4
- w_mlp_in: bfloat16 [8, 3072, 6144], P('section', None, 'sp'), may hold values from -0.109375 to 0.109375
- w_attn_out: bfloat16 [8, 2048, 3072], P('section', 'sp'), may hold values from -0.125 to 0.125
- w_mlp_out: bfloat16 [8, 6144, 3072], P('section', 'sp'), may hold values from -0.078125 to 0.078125
- kv_cache: bfloat16 [8, 2, 512, 2048], P('section', None, None, 'sp'), may hold values from -130 to 130
Outputs:
- slots_out: bfloat16 [8, 64, 3072], P('section', 'sp')
- kv_cache_out: bfloat16 [8, 2, 512, 2048], P('section', None, None, 'sp')
Inputs may be any that keep to these rules, and one draw needn't show every extreme that they name: `patch_of_slot`: each patch id names exactly one slot.
All inputs are finite; a program needn't handle non-finite values.
Results may differ from a plain program's by a relative error of at most 0.012.
The roundings to bfloat16 on the way count: a program that leaves them out, or rounds other values in their place, can miss the bound.
Values may be sent and summed in bfloat16 or wider, within the bound.
A program may use at most 128 MiB of HBM per device.

v0:
```python
import math

import jax
import jax.numpy as jnp
from jax import lax
from jax.sharding import PartitionSpec as P

HD = 128
ROUNDS = 2


def shifted_2(x, axis, by):
    length = lax.axis_size(axis)
    return lax.ppermute(x, axis, [(i, (i + by) % length) for i in range(length)])


def slot_labels(patch_of_slot, step_of_slot, section_id, sections, round_id):
    anchor = section_id - round_id
    wrapped = (anchor < 0).astype(jnp.int32)
    anchor = anchor + wrapped * sections
    patch_id = lax.dynamic_index_in_dim(patch_of_slot, anchor, 0, keepdims=False)
    timestep = lax.dynamic_index_in_dim(step_of_slot, anchor, 0, keepdims=False) + wrapped
    return (patch_id, timestep)


def modulate(slot, table, timestep):
    factors = lax.dynamic_index_in_dim(table, timestep, 0, keepdims=False).astype(jnp.float32)
    wide = slot.astype(jnp.float32)
    center = wide - jnp.mean(wide, axis=-1, keepdims=True)
    spread = jnp.mean(center * center, axis=-1, keepdims=True)
    normed = (center * lax.rsqrt(spread + 1e-06) * (1.0 + factors[1]) + factors[0]).astype(
        jnp.bfloat16
    )
    return (normed, factors[2])


def head_norm(part, gain):
    rows = part.shape[0]
    wide = part.astype(jnp.float32).reshape(rows, -1, HD)
    power = jnp.mean(wide * wide, axis=-1, keepdims=True)
    normed = wide * lax.rsqrt(power + 1e-06) * gain.astype(jnp.float32)
    return normed.astype(jnp.bfloat16).reshape(rows, -1)


def mix(normed, patch_id, keys, values, qkv_weight, norm_gain, inner_weight):
    patch_rows = normed.shape[0]
    projected = jnp.einsum(
        "rd,dce->rce", normed, qkv_weight, preferred_element_type=jnp.float32
    ).astype(jnp.bfloat16)
    query_normed = head_norm(projected[:, 0], norm_gain[0])
    key_normed = head_norm(projected[:, 1], norm_gain[1])
    first_row = patch_id * patch_rows
    keys = lax.dynamic_update_slice_in_dim(keys, key_normed, first_row, 0)
    values = lax.dynamic_update_slice_in_dim(values, projected[:, 2], first_row, 0)
    local_heads = qkv_weight.shape[2] // HD
    queries = query_normed.reshape(patch_rows, local_heads, HD)
    key_heads = keys.reshape(keys.shape[0], local_heads, HD)
    value_heads = values.reshape(values.shape[0], local_heads, HD)
    scores = jnp.einsum(
        "rhd,thd->hrt", queries, key_heads, preferred_element_type=jnp.float32
    ) / math.sqrt(HD)
    shifted = jnp.exp(scores - jnp.max(scores, axis=-1, keepdims=True))
    weights = (shifted / jnp.sum(shifted, axis=-1, keepdims=True)).astype(jnp.bfloat16)
    attention = jnp.einsum(
        "hrt,thd->rhd", weights, value_heads, preferred_element_type=jnp.float32
    ).astype(jnp.bfloat16)
    attention = attention.reshape(patch_rows, local_heads * HD)
    activity = jax.nn.gelu(
        jnp.dot(normed, inner_weight, preferred_element_type=jnp.float32), approximate=True
    ).astype(jnp.bfloat16)
    return (attention, activity, keys, values)


def shards(
    slots,
    patch_of_slot,
    step_of_slot,
    modulation,
    w_qkv,
    qk_scale,
    w_mlp_in,
    w_attn_out,
    w_mlp_out,
    kv_cache,
):
    sections = lax.axis_size("section")
    section_id = lax.axis_index("section")
    table = modulation[0]
    qkv_weight = w_qkv[0]
    norm_gain = qk_scale[0]
    inner_weight = w_mlp_in[0]
    attention_weight = w_attn_out[0]
    outer_weight = w_mlp_out[0]
    keys = kv_cache[0, 0]
    values = kv_cache[0, 1]
    current = slots[0]
    for round_id in range(ROUNDS):
        patch_id, timestep = slot_labels(
            patch_of_slot, step_of_slot, section_id, sections, round_id
        )
        normed, gate = modulate(current, table, timestep)
        gathered = lax.all_gather(normed, "sp", axis=0, tiled=True)
        attention, activity, keys, values = mix(
            gathered, patch_id, keys, values, qkv_weight, norm_gain, inner_weight
        )
        summed = lax.psum_scatter(
            jnp.dot(attention, attention_weight, preferred_element_type=jnp.float32)
            + jnp.dot(activity, outer_weight, preferred_element_type=jnp.float32),
            "sp",
            scatter_dimension=0,
            tiled=True,
        )
        current = (current.astype(jnp.float32) + gate * summed).astype(jnp.bfloat16)
        current = shifted_2(current, "section", 1)
    return (current[None], jnp.stack([keys, values])[None])


def solution(mesh):
    return jax.shard_map(
        shards,
        mesh=mesh,
        in_specs=(
            P("section", "sp", None),
            P(),
            P(),
            P("section", None, None, None),
            P("section", None, None, "sp"),
            P("section", None, None),
            P("section", None, "sp"),
            P("section", "sp", None),
            P("section", "sp", None),
            P("section", None, None, "sp"),
        ),
        out_specs=(P("section", "sp", None), P("section", None, None, "sp")),
        check_vma=False,
    )
```

profile of v0, /device:TPU:0, one launch (start us, length us, event | category | flops | bytes accessed | tf_op | source)
XLA Modules:
  0.0 167.5 jit_solution(4243457292436387553)
XLA Ops:
  7.2 1.5 fusion.120
  10.0 1.0 dynamic-slice_convert_fusion
  11.1 1.0 convert_reduce_fusion.1
  12.1 1.1 fusion.78
  13.2 1.0 fusion.81
  14.3 8.0 %all_gather.6 = bf16[64,3072]{1,0:T(8,128)(2,1)S(1)} all-gather(bf16[16,3072]{1,0:T(8,128)(2,1)S(1)} %fusion.81), channel_id=1, replica_groups=mesh['section'=8,'sp'=4] {'sp'}, dimensions={0}, use_global_device_ids=true | all-gather | bytes 491520 | tf_op jit(solution)/shard_map/all_gather | solution.py:102
  22.2 0.7 copy-done.1
  23.0 5.4 %fusion.20 = bf16[64,3,512]{2,0,1:T(8,128)(2,1)S(1)} fusion(bf16[1,3072,3,512]{3,1,2,0:T(8,128)(2,1)} %param.14, bf16[64,3072]{1,0:T(8,128)(2,1)S(1)} %all_gather.6), kind=kOutput, calls=%fused_computation.24 | convolution fusion | flops 604078080 | bytes 10027008 | tf_op jit(solution)/shard_map/rd,dce->rce/dot_general | solution.py:47
  28.4 0.7 convert_multiply_fusion.1
  29.0 0.7 slice_convert_fusion.1
  29.7 0.9 mul.239
  30.6 0.8 reduce_sum.93
  31.4 0.8 add_rsqrt_fusion.2
  32.7 1.3 bitcast_convert_fusion.1
  34.6 2.3 %slice_bitcast_fusion = (bf16[512,512]{1,0:T(8,128)(2,1)}, bf16[512,512]{1,0:T(8,128)(2,1)}) fusion(bf16[1,2,512,512]{3,2,1,0:T(8,128)(2,1)} %param.19), kind=kLoop, calls=%fused_computation.43 | loop fusion | bytes 2097152 | tf_op jit(solution)/shard_map/squeeze | solution.py:94
  36.9 0.9 reshape.147
  38.6 0.9 multiply_convert_fusion.1
  39.6 1.3 fusion.99
  41.0 1.3 convolution_multiply_fusion.1
  42.3 0.8 copy-done.3
  43.3 2.0 %fusion.26 = bf16[4,8,8,128]{3,2,1,0:T(8,128)(2,1)S(1)} fusion(f32[4,64]{1,0:T(4,128)S(1)} %fusion.122, f32[4,64,512]{2,1,0:T(8,128)} %copy-done.3, bf16[512,512]{1,0:T(8,128)(2,1)} %get-tuple-element.9), kind=kOutput, calls=%fused_computation.28 | convolution fusion | flops 33981184 | bytes 1115136 | tf_op jit(solution)/shard_map/hrt,thd->rhd/dot_general | solution.py:64
  45.4 10.8 %fusion.4 = f32[64,3072]{1,0:T(8,128)} fusion(bf16[1,1536,3072]{2,1,0:T(8,128)(2,1)} %param.18, bf16[64,3072]{1,0:T(8,128)(2,1)} %copy-done.1, bf16[1,3072,1536]{2,1,0:T(8,128)(2,1)} %param.16), kind=kOutput, calls=%fused_computation.4 | convolution fusion | flops 1208844288 | bytes 20054016 | tf_op jit(solution)/shard_map/dot_general | solution.py:108
  56.2 2.7 %convolution_add_fusion.1 = f32[64,3072]{1,0:T(8,128)} fusion(f32[64,3072]{1,0:T(8,128)} %fusion.4, bf16[1,512,3072]{2,1,0:T(8,128)(2,1)S(1)} %copy-done, bf16[4,8,8,128]{3,2,1,0:T(8,128)(2,1)S(1)} %fusion.26), kind=kOutput, calls=%fused_computation.15 | convolution fusion | flops 201523200 | bytes 4784128 | tf_op jit(solution)/shard_map/dot_general | solution.py:107
  58.9 24.2 %reduce-scatter.3.cloned.1.call-done = f32[16,3072]{1,0:T(8,128)} async-done(((f32[64,3072]{1,0:T(8,128)}), f32[16,3072]{1,0:T(8,128)}) %reduce-scatter.3.cloned.1.call-update) | async-done | bytes 196624 | tf_op jit(solution)/shard_map/reduce_scatter | solution.py:106
  83.1 1.0 fusion.82
  84.1 1.5 collective-permute-start
  86.3 5.2 %collective-permute-done = bf16[16,3072]{1,0:T(8,128)(2,1)S(1)} collective-permute-done((bf16[16,3072]{1,0:T(8,128)(2,1)S(1)}, bf16[16,3072]{1,0:T(8,128)(2,1)S(1)}, u32[]{:S(2)}, u32[]{:S(2)}) %collective-permute-start) | collective-permute-done | bytes 98336 | tf_op jit(solution)/shard_map/ppermute | solution.py:14
  91.9 6.3 %all_gather.7 = bf16[64,3072]{1,0:T(8,128)(2,1)S(1)} all-gather(bf16[16,3072]{1,0:T(8,128)(2,1)S(1)} %fusion.77), channel_id=1, replica_groups=mesh['section'=8,'sp'=4] {'sp'}, dimensions={0}, use_global_device_ids=true | all-gather | bytes 491520 | tf_op jit(solution)/shard_map/all_gather | solution.py:102
  98.3 0.7 copy-done.2
  99.0 5.4 %fusion.23 = bf16[64,3,512]{2,0,1:T(8,128)(2,1)S(1)} fusion(bf16[1,3072,3,512]{3,1,2,0:T(8,128)(2,1)} %param.14, bf16[64,3072]{1,0:T(8,128)(2,1)S(1)} %all_gather.7), kind=kOutput, calls=%fused_computation.25 | convolution fusion | flops 604078080 | bytes 10027008 | tf_op jit(solution)/shard_map/rd,dce->rce/dot_general | solution.py:47
  104.4 0.7 convert_multiply_fusion
  105.1 0.7 slice_convert_fusion
  105.7 10.8 %fusion.2 = f32[64,3072]{1,0:T(8,128)} fusion(bf16[1,1536,3072]{2,1,0:T(8,128)(2,1)} %param.18, bf16[64,3072]{1,0:T(8,128)(2,1)} %copy-done.2, bf16[1,3072,1536]{2,1,0:T(8,128)(2,1)} %param.16), kind=kOutput, calls=%fused_computation.2 | convolution fusion | flops 1208844288 | bytes 20054016 | tf_op jit(solution)/shard_map/dot_general | solution.py:108
  116.5 1.6 mul.270
  118.1 1.0 reduce_sum.98
  119.2 1.6 reshape.151
  120.8 1.0 multiply_reduce_fusion
  121.9 1.0 multiply_convert_fusion
  123.0 0.7 fusion.98
  123.7 1.3 convolution_multiply_fusion
  125.0 0.8 copy-done.4
  126.1 1.9 %fusion.27 = bf16[4,8,8,128]{3,2,1,0:T(8,128)(2,1)S(1)} fusion(f32[4,64]{1,0:T(4,128)S(1)} %fusion.123, f32[4,64,512]{2,1,0:T(8,128)} %copy-done.4, bf16[512,512]{1,0:T(8,128)(2,1)} %get-tuple-element.7), kind=kOutput, calls=%fused_computation.29 | convolution fusion | flops 33981184 | bytes 1115136 | tf_op jit(solution)/shard_map/hrt,thd->rhd/dot_general | solution.py:64
  128.0 2.7 %convolution_add_fusion = f32[64,3072]{1,0:T(8,128)} fusion(f32[64,3072]{1,0:T(8,128)} %fusion.2, bf16[1,512,3072]{2,1,0:T(8,128)(2,1)S(1)} %copy-done, bf16[4,8,8,128]{3,2,1,0:T(8,128)(2,1)S(1)} %fusion.27), kind=kOutput, calls=%fused_computation.14 | convolution fusion | flops 201523200 | bytes 4784128 | tf_op jit(solution)/shard_map/dot_general | solution.py:107
  130.7 21.0 %reduce-scatter.5.cloned.1.call-done = f32[16,3072]{1,0:T(8,128)} async-done(((f32[64,3072]{1,0:T(8,128)}), f32[16,3072]{1,0:T(8,128)}) %reduce-scatter.5.cloned.1.call-update) | async-done | bytes 196624 | tf_op jit(solution)/shard_map/reduce_scatter | solution.py:106
  151.7 1.0 fusion.83
  152.7 1.5 collective-permute-start.1
  154.2 2.3 %maximum_bitcast_fusion = bf16[1,2,512,512]{3,2,1,0:T(8,128)(2,1)} fusion(bf16[1,512,512]{2,1,0:T(8,128)(2,1)} %bitcast.182, bf16[1,512,512]{2,1,0:T(8,128)(2,1)} %bitcast.181), kind=kLoop, calls=%fused_computation.30 | loop fusion | flops 524288 | bytes 2097152 | tf_op jit(solution)/shard_map/broadcast_in_dim | solution.py:115
  156.5 3.6 %collective-permute-done.1 = bf16[16,3072]{1,0:T(8,128)(2,1)S(1)} collective-permute-done((bf16[16,3072]{1,0:T(8,128)(2,1)S(1)}, bf16[16,3072]{1,0:T(8,128)(2,1)S(1)}, u32[]{:S(2)}, u32[]{:S(2)}) %collective-permute-start.1) | collective-permute-done | bytes 98336 | tf_op jit(solution)/shard_map/ppermute | solution.py:14
  (35 shorter events, 3.4 us)
Async XLA Ops:
  7.2 49.0 %copy-start = (bf16[1,512,3072]{2,1,0:T(8,128)(2,1)S(1)}, bf16[1,512,3072]{2,1,0:T(8,128)(2,1)}, u32[]{:S(2)}) copy-start(bf16[1,512,3072]{2,1,0:T(8,128)(2,1)} %param.17) | copy-start | bytes 9437188
  7.2 76.0 %reduce-scatter.3.cloned.1.call-start = ((), (), s32[]{:S(2)}) async-start(), calls=%async_computation.2 | async-start | bytes 983040 | tf_op jit(solution)/shard_map/reduce_scatter | solution.py:106
  22.2 0.7 copy-start.1
  42.3 0.8 copy-start.3
  45.4 37.8 %copy-start.5 = (bf16[1,16,3072]{2,1,0:T(8,128)(2,1)S(1)}, bf16[1,16,3072]{2,1,0:T(8,128)(2,1)}, u32[]{:S(2)}) copy-start(bf16[1,16,3072]{2,1,0:T(8,128)(2,1)} %param.10) | copy-start | bytes 294916
  58.9 92.8 %reduce-scatter.5.cloned.1.call-start = ((), (), s32[]{:S(2)}) async-start(), calls=%async_computation.3 | async-start | bytes 983040 | tf_op jit(solution)/shard_map/reduce_scatter | solution.py:106
  84.1 7.4 %collective-permute-start = (bf16[16,3072]{1,0:T(8,128)(2,1)S(1)}, bf16[16,3072]{1,0:T(8,128)(2,1)S(1)}, u32[]{:S(2)}, u32[]{:S(2)}) collective-permute-start(bf16[16,3072]{1,0:T(8,128)(2,1)S(1)} %fusion.82), channel_id=1, source_target_pairs={{0,4},{4,8},{8,12},{12,16},{16,20},{20,24},{24,28},{28,0},{1,5},{5... | collective-permute-start | bytes 294920 | tf_op jit(solution)/shard_map/ppermute | solution.py:14
  98.3 0.7 copy-start.2
  105.7 16.1 %copy-start.7 = (f32[128]{0:T(128)S(1)}, f32[128]{0:T(128)}, u32[]{:S(2)}) copy-start(f32[128]{0:T(128)} %get-tuple-element.20) | copy-start | bytes 1540
  105.7 17.3 %copy-start.6 = (f32[512]{0:T(512)S(1)}, f32[512]{0:T(512)}, u32[]{:S(2)}) copy-start(f32[512]{0:T(512)} %broadcast_bitcast_fusion) | copy-start | bytes 6148
  125.0 0.8 copy-start.4
  152.7 7.4 %collective-permute-start.1 = (bf16[16,3072]{1,0:T(8,128)(2,1)S(1)}, bf16[16,3072]{1,0:T(8,128)(2,1)S(1)}, u32[]{:S(2)}, u32[]{:S(2)}) collective-permute-start(bf16[16,3072]{1,0:T(8,128)(2,1)S(1)} %fusion.83), channel_id=1, source_target_pairs={{0,4},{4,8},{8,12},{12,16},{16,20},{20,24},{24,28},{28,0},{1,5},{5... | collective-permute-start | bytes 294920 | tf_op jit(solution)/shard_map/ppermute | solution.py:14
Sparse Core Ops, SparseCore 0:
  59.0 24.0 reduce-scatter.2
  130.9 20.8 reduce-scatter.4
where the time goes:
time: 169 us; the launch traced here: 168 us
  waiting for transfers between devices  54 us (32%)
  matrix products  44.3 us (26%)
  other arithmetic  21.6 us (13%)
  between operations  16.8 us (10%)
  blocking collectives  14.3 us (8%)
  local copies, waits for them, and re-layouts  13.4 us (8%)
  starting transfers between devices  3.14 us (2%)
    reduce_scatter x2, waiting for transfers between devices, shards(): lax.psum_scatter(jnp.dot(attention, attention_weight, preferred_element_t...  45.2 us
    dot_general x2, matrix products, shards(): jnp.dot(activity, outer_weight, preferred_element_type=jnp.float32)  21.6 us
    all_gather x2, blocking collectives, shards(): gathered = lax.all_gather(normed, 'sp', axis=0, tiled=True)  14.3 us
    dot_general x2, matrix products, mix(): jnp.einsum('rd,dce->rce', normed, qkv_weight, preferred_element_type=jnp....  10.8 us
    ppermute x2, waiting for transfers between devices, shifted_2(): lax.ppermute(x, axis, [(i, (i + by) % length) for i in range(length)])  8.75 us
    dot_general x2, matrix products, shards(): jnp.dot(attention, attention_weight, preferred_element_type=jnp.float32)  5.36 us
    dot_general x2, matrix products, mix(): jnp.einsum('hrt,thd->rhd', weights, value_heads, preferred_element_type=j...  3.95 us
    unnamed x17, local copies, waits for them, and re-layouts  3.75 us
  transfers between devices with their start and end apart: 4, of which 4 were waited for; matrix products, arithmetic and copies ran while one was open for 1% of the time, Pallas kernels for 0%

commit v1 on v0

v1 whole, which is shorter than its diff:
```python
import functools
import math

import jax
import jax.numpy as jnp
from jax import lax
from jax.experimental import pallas as pl
from jax.experimental.pallas import tpu as pltpu
from jax.sharding import PartitionSpec as P

HD = 128
ROUNDS = 2
F32 = jnp.float32
BF16 = jnp.bfloat16
MESH = pl.DeviceIdType.MESH


def divides(total, wanted):
    return max(size for size in range(128, wanted + 1, 128) if total % size == 0)


def kernel(sections, peers, patch_ref, step_ref, slots_ref, mod_ref, gain_ref,
           qkv_hbm, inner_hbm, attn_hbm, outer_hbm, kv_hbm,
           x_out, kv_out,
           qkv, inner, attn_w, outer, kv, gathered, landed, part, whole, fresh, arrived,
           h_buf, a_buf, act_buf, factors, load_sem, kv_sem, out_sem,
           ag_send, ag_recv, rs_send, rs_recv, sh_send, sh_recv):
    rows, width = slots_ref.shape
    total_rows = peers * rows
    heads = qkv.shape[2] // HD
    hidden = inner.shape[1]
    tokens = kv.shape[1]
    chunks = rs_send.shape[1]
    cut = width // chunks
    in_cut = divides(hidden, 512)
    in_chunks = hidden // in_cut
    me = lax.axis_index("sp")
    sid = lax.axis_index("section")
    following = lax.rem(sid + 1, sections)
    previous = lax.rem(sid + sections - 1, sections)

    loads = []

    def load(source, target):
        copy = pltpu.make_async_copy(source, target, load_sem.at[len(loads)])
        loads.append(copy)
        return copy

    qkv_loads = [load(qkv_hbm.at[i], qkv.at[i]) for i in range(3)]
    inner_loads = [
        load(inner_hbm.at[:, pl.ds(i * in_cut, in_cut)], inner.at[:, pl.ds(i * in_cut, in_cut)])
        for i in range(in_chunks)
    ]
    out_loads = []
    for c in range(chunks):
        span = pl.ds(c * cut, cut)
        out_loads.append(
            (load(attn_hbm.at[:, span], attn_w.at[:, span]),
             load(outer_hbm.at[:, span], outer.at[:, span]))
        )
    kv_load = pltpu.make_async_copy(kv_hbm, kv, kv_sem)
    for copy in qkv_loads:
        copy.start()
    kv_load.start()
    for copy in loads[3:]:
        copy.start()

    barrier = pltpu.get_barrier_semaphore()
    for k in range(1, peers):
        pl.semaphore_signal(barrier, inc=1, device_id={"sp": lax.rem(me + k, peers)}, device_id_type=MESH)
    for other in (following, previous):
        pl.semaphore_signal(barrier, inc=1, device_id={"section": other}, device_id_type=MESH)
    pl.semaphore_wait(barrier, peers - 1 + 2)

    sends = []
    gathers = [[], []]
    for k in range(1, peers):
        copy = pltpu.make_async_remote_copy(
            src_ref=slots_ref, dst_ref=gathered.at[0, me],
            send_sem=ag_send.at[0, 0, k], recv_sem=ag_recv.at[0, 0, k],
            device_id={"sp": lax.rem(me + k, peers)}, device_id_type=MESH)
        copy.start()
        gathers[0].append(copy)
        sends.append(copy)
    gathered[0, me] = slots_ref[...]

    for r in range(ROUNDS):
        anchor = sid - r
        wrapped = (anchor < 0).astype(jnp.int32)
        anchor = anchor + wrapped * sections
        patch = patch_ref[anchor]
        step = step_ref[anchor] + wrapped
        table_rows = lax.broadcasted_iota(jnp.int32, (mod_ref.shape[1], width), 0)
        for i in range(3):
            picked = jnp.where(table_rows == step, mod_ref[i].astype(F32), 0.0)
            factors[i : i + 1, :] = jnp.sum(picked, axis=0, keepdims=True)
        shift = factors[0:1, :]
        scale = 1.0 + factors[1:2, :]

        if r > 0:
            for c in range(chunks):
                span = pl.ds(c * cut, cut)
                shifts[c].wait_recv()
                for k in range(1, peers):
                    copy = pltpu.make_async_remote_copy(
                        src_ref=gathered.at[r, me, :, span], dst_ref=gathered.at[r, me, :, span],
                        send_sem=ag_send.at[r, c, k], recv_sem=ag_recv.at[r, c, k],
                        device_id={"sp": lax.rem(me + k, peers)}, device_id_type=MESH)
                    copy.start()
                    gathers[r].append(copy)
                    sends.append(copy)
        for copy in gathers[r]:
            copy.wait_recv()
        for n in range(peers):
            wide = gathered[r, n].astype(F32)
            center = wide - jnp.mean(wide, axis=-1, keepdims=True)
            spread = jnp.mean(center * center, axis=-1, keepdims=True)
            h_buf[n * rows : (n + 1) * rows, :] = (
                center * lax.rsqrt(spread + 1e-06) * scale + shift
            ).astype(BF16)

        made = []
        for i in range(3):
            if r == 0:
                qkv_loads[i].wait()
            made.append(jnp.dot(h_buf[...], qkv[i], preferred_element_type=F32).astype(BF16))
        if r == 0:
            kv_load.wait()

        def head_norm(value, head, which):
            one = value[:, head * HD : (head + 1) * HD].astype(F32)
            power = jnp.mean(one * one, axis=-1, keepdims=True)
            return (one * lax.rsqrt(power + 1e-06) * gain_ref[which : which + 1, :].astype(F32)).astype(BF16)

        for head in range(heads):
            lanes = slice(head * HD, (head + 1) * HD)
            query = head_norm(made[0], head, 0)
            key = head_norm(made[1], head, 1)
            value = made[2][:, lanes]
            for p in range(tokens // total_rows):
                there = slice(p * total_rows, (p + 1) * total_rows)
                hit = jnp.broadcast_to(patch, (total_rows, HD)) == p
                kv[0, there, lanes] = jnp.where(hit, key.astype(F32), kv[0, there, lanes].astype(F32)).astype(BF16)
                kv[1, there, lanes] = jnp.where(hit, value.astype(F32), kv[1, there, lanes].astype(F32)).astype(BF16)
            scores = lax.dot_general(
                query, kv[0, :, lanes], (((1,), (1,)), ((), ())), preferred_element_type=F32
            ) / math.sqrt(HD)
            raised = jnp.exp(scores - jnp.max(scores, axis=-1, keepdims=True))
            probs = (raised / jnp.sum(raised, axis=-1, keepdims=True)).astype(BF16)
            a_buf[:, lanes] = jnp.dot(probs, kv[1, :, lanes], preferred_element_type=F32).astype(BF16)
        if r == ROUNDS - 1:
            kv_store = pltpu.make_async_copy(kv, kv_out, out_sem)
            kv_store.start()

        for i in range(in_chunks):
            if r == 0:
                inner_loads[i].wait()
            span = slice(i * in_cut, (i + 1) * in_cut)
            act_buf[:, span] = jax.nn.gelu(
                jnp.dot(h_buf[...], inner[:, span], preferred_element_type=F32), approximate=True
            ).astype(BF16)

        reduces = []
        for c in range(chunks):
            if r == 0:
                out_loads[c][0].wait()
                out_loads[c][1].wait()
            lanes = slice(c * cut, (c + 1) * cut)
            span = pl.ds(c * cut, cut)
            share = jnp.dot(a_buf[...], attn_w[:, lanes], preferred_element_type=F32)
            share = share + jnp.dot(act_buf[...], outer[:, lanes], preferred_element_type=F32)
            for n in range(peers):
                block = share[n * rows : (n + 1) * rows, :]
                whole[n, :, lanes] = block
                part[r, n, :, lanes] = block.astype(BF16)
            group = []
            for k in range(1, peers):
                to = lax.rem(me + k, peers)
                copy = pltpu.make_async_remote_copy(
                    src_ref=part.at[r, to, :, span], dst_ref=landed.at[r, k, :, span],
                    send_sem=rs_send.at[r, c, k], recv_sem=rs_recv.at[r, c, k],
                    device_id={"sp": to}, device_id_type=MESH)
                copy.start()
                group.append(copy)
                sends.append(copy)
            reduces.append(group)

        shifts = []
        for c in range(chunks):
            lanes = slice(c * cut, (c + 1) * cut)
            span = pl.ds(c * cut, cut)
            for copy in reduces[c]:
                copy.wait_recv()
            summed = whole[me, :, lanes]
            for k in range(1, peers):
                summed = summed + landed[r, k, :, lanes].astype(F32)
            fresh[r, :, lanes] = (
                gathered[r, me, :, lanes].astype(F32) + factors[2:3, lanes] * summed
            ).astype(BF16)
            target = gathered.at[r + 1, me, :, span] if r < ROUNDS - 1 else arrived.at[:, span]
            copy = pltpu.make_async_remote_copy(
                src_ref=fresh.at[r, :, span], dst_ref=target,
                send_sem=sh_send.at[r, c], recv_sem=sh_recv.at[r, c],
                device_id={"section": following}, device_id_type=MESH)
            copy.start()
            shifts.append(copy)
            sends.append(copy)

    for copy in shifts:
        copy.wait_recv()
    x_out[...] = arrived[...]
    kv_store.wait()
    for copy in sends:
        copy.wait_send()


def shards(sections, peers, slots, patch_of_slot, step_of_slot, modulation, w_qkv, qk_scale,
           w_mlp_in, w_attn_out, w_mlp_out, kv_cache):
    rows, width = slots.shape[1:]
    local = w_qkv.shape[3]
    hidden = w_mlp_in.shape[2]
    total_rows = peers * rows
    tokens = kv_cache.shape[2]
    chunks = width // divides(width, 768)
    loads = 3 + hidden // divides(hidden, 512) + 2 * chunks
    dma = pltpu.SemaphoreType.DMA
    vmem = pl.BlockSpec(memory_space=pltpu.VMEM)
    smem = pl.BlockSpec(memory_space=pltpu.SMEM)
    anywhere = pl.BlockSpec(memory_space=pl.ANY)
    x, kv = pl.pallas_call(
        functools.partial(kernel, sections, peers),
        out_shape=(
            jax.ShapeDtypeStruct((rows, width), BF16),
            jax.ShapeDtypeStruct(kv_cache.shape[1:], BF16),
        ),
        in_specs=[smem, smem, vmem, vmem, vmem] + [anywhere] * 5,
        out_specs=(vmem, anywhere),
        scratch_shapes=[
            pltpu.VMEM((3, width, local), BF16),
            pltpu.VMEM((width, hidden), BF16),
            pltpu.VMEM((local, width), BF16),
            pltpu.VMEM((hidden, width), BF16),
            pltpu.VMEM((2, tokens, local), BF16),
            pltpu.VMEM((ROUNDS, peers, rows, width), BF16),
            pltpu.VMEM((ROUNDS, peers, rows, width), BF16),
            pltpu.VMEM((ROUNDS, peers, rows, width), BF16),
            pltpu.VMEM((peers, rows, width), F32),
            pltpu.VMEM((ROUNDS, rows, width), BF16),
            pltpu.VMEM((rows, width), BF16),
            pltpu.VMEM((total_rows, width), BF16),
            pltpu.VMEM((total_rows, local), BF16),
            pltpu.VMEM((total_rows, hidden), BF16),
            pltpu.VMEM((8, width), F32),
            dma((loads,)),
            dma,
            dma,
            dma((ROUNDS, chunks, peers)),
            dma((ROUNDS, chunks, peers)),
            dma((ROUNDS, chunks, peers)),
            dma((ROUNDS, chunks, peers)),
            dma((ROUNDS, chunks)),
            dma((ROUNDS, chunks)),
        ],
        compiler_params=pltpu.CompilerParams(
            collective_id=0, has_side_effects=True, vmem_limit_bytes=60 * 1024 * 1024
        ),
    )(
        patch_of_slot, step_of_slot, slots[0], jnp.transpose(modulation[0], (1, 0, 2)), qk_scale[0],
        jnp.transpose(w_qkv[0], (1, 0, 2)), w_mlp_in[0], w_attn_out[0], w_mlp_out[0], kv_cache[0],
    )
    return (x[None], kv[None])


def solution(mesh):
    return jax.shard_map(
        functools.partial(shards, mesh.shape["section"], mesh.shape["sp"]),
        mesh=mesh,
        in_specs=(
            P("section", "sp", None),
            P(),
            P(),
            P("section", None, None, None),
            P("section", None, None, "sp"),
            P("section", None, None),
            P("section", None, "sp"),
            P("section", "sp", None),
            P("section", "sp", None),
            P("section", None, None, "sp"),
        ),
        out_specs=(P("section", "sp", None), P("section", None, None, "sp")),
        check_vma=False,
    )
```

time: 169 us -> 54.3 us (0.32)
  waiting for transfers between devices: 54 us -> 0 us
  Pallas kernels: 0 us -> 49.6 us
  matrix products: 44.3 us -> 0 us
  other arithmetic: 21.6 us -> 0 us
  between operations: 16.8 us -> 0.64 us
  blocking collectives: 14.3 us -> 0 us
  local copies, waits for them, and re-layouts: 13.4 us -> 3.8 us
  starting transfers between devices: 3.14 us -> 0 us
    pallas_call x0 -> x1, Pallas kernels: none -> 49.6 us  [shards(): pl.pallas_call(functools.partial(kernel, sections, peers), out_shape=(jax...]
    reduce_scatter x2 -> x0, waiting for transfers between devices: 45.2 us -> none  [shards(): lax.psum_scatter(jnp.dot(attention, attention_weight, preferred_element_t...]
    dot_general x10 -> x0, matrix products: 44.3 us -> none  [the longest x2 21.6 us: shards(): jnp.dot(activity, outer_weight, preferred_element_type=jnp.float32)]
    all_gather x2 -> x0, blocking collectives: 14.3 us -> none  [shards(): gathered = lax.all_gather(normed, 'sp', axis=0, tiled=True)]
    ppermute x2 -> x0, waiting for transfers between devices: 8.75 us -> none  [shifted_2(): lax.ppermute(x, axis, [(i, (i + by) % length) for i in range(length)])]
    convert_element_type x9 -> x0, other arithmetic: 7.33 us -> none  [the longest x2 1.93 us: head_norm(): return normed.astype(jnp.bfloat16).reshape(rows, -1)]
    reduce_sum x8 -> x0, other arithmetic: 5.46 us -> none  [the longest x4 2.98 us: head_norm(): power = jnp.mean(wide * wide, axis=-1, keepdims=True)]
    mul x5 -> x0, local copies, waits for them, and re-layouts: 3.36 us -> none  [the longest x2 2.54 us: head_norm(): power = jnp.mean(wide * wide, axis=-1, keepdims=True)]
  transfers between devices with their start and end apart: 4 -> 0, of which waited for: 4 -> 0; matrix products, arithmetic and copies ran while one was open for 1% -> 0% of each run, Pallas kernels for 0% -> 0%
where the time goes in v1:
time: 54.3 us; the launch traced here: 54.1 us
  Pallas kernels  49.6 us (91%)
  local copies, waits for them, and re-layouts  3.8 us (7%)
  between operations  0.64 us (1%)
    pallas_call x1, Pallas kernels, shards(): pl.pallas_call(functools.partial(kernel, sections, peers), out_shape=(jax...  49.6 us
    unnamed x2, local copies, waits for them, and re-layouts  3.8 us

profile of v1, /device:TPU:0, one launch (start us, length us, event | category | flops | bytes accessed | tf_op | source)
XLA Modules:
  0.0 54.1 jit_solution(10292855600518235826)
XLA Ops:
  0.6 49.6 %shard_map.113 = (bf16[16,3072]{1,0:T(8,128)(2,1)}, bf16[2,512,512]{2,1,0:T(8,128)(2,1)}) custom-call(s32[8]{0:T(128)} %patch_ref.1, s32[8]{0:T(128)} %step_ref.1, bf16[16,3072]{1,0:T(8,128)(2,1)} %bitcast.21, bf16[3,28,3072]{2,1,0:T(8,128)(2,1)} %bitcast.20, bf16[2,128]{1,0:T(2,128)(2,1)} %bitcast.23, bf16[3,3072,512]{2,1,0:T(8,128)(2,1)} %bitcast.14, ...), custom_call_target="tpu_custom_call" | custom-call | tf_op jit(solution)/shard_map/pallas_call | solution.py:230
  50.3 1.5 %copy.14 = bf16[1,16,3072]{2,1,0:T(8,128)(2,1)} copy(bf16[1,16,3072]{2,1,0:T(8,128)(2,1)} %bitcast.22) | data formatting | bytes 196608
  51.8 2.3 %copy.15 = bf16[1,2,512,512]{3,2,1,0:T(8,128)(2,1)} copy(bf16[1,2,512,512]{3,2,1,0:T(8,128)(2,1)} %bitcast.19) | data formatting | bytes 2097152

commit v2 on v1

--- a/solution.py
+++ b/solution.py
@@ -22,7 +22,7 @@
 def kernel(sections, peers, patch_ref, step_ref, slots_ref, mod_ref, gain_ref,
            qkv_hbm, inner_hbm, attn_hbm, outer_hbm, kv_hbm,
            x_out, kv_out,
-           qkv, inner, attn_w, outer, kv, gathered, landed, part, whole, fresh, arrived,
+           qkv, inner, attn_w, outer, kv, gathered, landed, paired, part, mid, whole, fresh, arrived,
            h_buf, a_buf, act_buf, factors, load_sem, kv_sem, out_sem,
            ag_send, ag_recv, rs_send, rs_recv, sh_send, sh_recv):
     rows, width = slots_ref.shape
@@ -35,6 +35,45 @@
     in_cut = divides(hidden, 512)
     in_chunks = hidden // in_cut
     me = lax.axis_index("sp")
+    groups = peers // 2
+    group = me // 2
+    core = lax.rem(me, 2)
+    partner = group * 2 + 1 - core
+
+    def alike(k):
+        return lax.rem(group + k, groups)
+
+    def spread_rows(r, c, source):
+        span = pl.ds(c * cut, cut)
+        across, beside = [], []
+        for k in range(1, groups):
+            across.append(remote(
+                source, gathered.at[r, me, :, span], ag_send.at[r, c, k], ag_recv.at[r, c, k],
+                {"sp": alike(k) * 2 + core}))
+        beside.append(remote(
+            source, gathered.at[r, me, :, span], ag_send.at[r, c, groups], ag_recv.at[r, c, groups],
+            {"sp": partner}))
+        return across, beside
+
+    def relay_rows(r, c, across, beside):
+        span = pl.ds(c * cut, cut)
+        for k in range(1, groups):
+            across[k - 1].wait_recv()
+            block = gathered.at[r, alike(groups - k) * 2 + core, :, span]
+            beside.append(remote(
+                block, block, ag_send.at[r, c, groups + k], ag_recv.at[r, c, groups + k],
+                {"sp": partner}))
+
+    sends = []
+
+    def remote(source, target, send_sem, recv_sem, device):
+        copy = pltpu.make_async_remote_copy(
+            src_ref=source, dst_ref=target, send_sem=send_sem, recv_sem=recv_sem,
+            device_id=device, device_id_type=MESH)
+        copy.start()
+        sends.append(copy)
+        return copy
+
     sid = lax.axis_index("section")
     following = lax.rem(sid + 1, sections)
     previous = lax.rem(sid + sections - 1, sections)
@@ -72,16 +111,7 @@
         pl.semaphore_signal(barrier, inc=1, device_id={"section": other}, device_id_type=MESH)
     pl.semaphore_wait(barrier, peers - 1 + 2)
 
-    sends = []
-    gathers = [[], []]
-    for k in range(1, peers):
-        copy = pltpu.make_async_remote_copy(
-            src_ref=slots_ref, dst_ref=gathered.at[0, me],
-            send_sem=ag_send.at[0, 0, k], recv_sem=ag_recv.at[0, 0, k],
-            device_id={"sp": lax.rem(me + k, peers)}, device_id_type=MESH)
-        copy.start()
-        gathers[0].append(copy)
-        sends.append(copy)
+    moves = [spread_rows(0, c, slots_ref.at[:, pl.ds(c * cut, cut)]) for c in range(chunks)]
     gathered[0, me] = slots_ref[...]
 
     for r in range(ROUNDS):
@@ -98,19 +128,19 @@
         scale = 1.0 + factors[1:2, :]
 
         if r > 0:
+            moves = []
             for c in range(chunks):
-                span = pl.ds(c * cut, cut)
                 shifts[c].wait_recv()
-                for k in range(1, peers):
-                    copy = pltpu.make_async_remote_copy(
-                        src_ref=gathered.at[r, me, :, span], dst_ref=gathered.at[r, me, :, span],
-                        send_sem=ag_send.at[r, c, k], recv_sem=ag_recv.at[r, c, k],
-                        device_id={"sp": lax.rem(me + k, peers)}, device_id_type=MESH)
-                    copy.start()
-                    gathers[r].append(copy)
-                    sends.append(copy)
-        for copy in gathers[r]:
-            copy.wait_recv()
+                moves.append(spread_rows(r, c, gathered.at[r, me, :, pl.ds(c * cut, cut)]))
+                if c > 0:
+                    relay_rows(r, c - 1, *moves[c - 1])
+            relay_rows(r, chunks - 1, *moves[chunks - 1])
+        else:
+            for c in range(chunks):
+                relay_rows(r, c, *moves[c])
+        for _, beside in moves:
+            for copy in beside:
+                copy.wait_recv()
         for n in range(peers):
             wide = gathered[r, n].astype(F32)
             center = wide - jnp.mean(wide, axis=-1, keepdims=True)
@@ -160,7 +190,23 @@
                 jnp.dot(h_buf[...], inner[:, span], preferred_element_type=F32), approximate=True
             ).astype(BF16)
 
-        reduces = []
+        pairs, reduces = [], []
+
+        def pass_on(c):
+            lanes = slice(c * cut, (c + 1) * cut)
+            span = pl.ds(c * cut, cut)
+            pairs[c].wait_recv()
+            crossing = []
+            for k in range(1, groups):
+                to = alike(k)
+                mid[r, k, :, lanes] = (
+                    whole[to * 2 + core, :, lanes] + paired[r, to, :, lanes].astype(F32)
+                ).astype(BF16)
+                crossing.append(remote(
+                    mid.at[r, k, :, span], landed.at[r, k, :, span],
+                    rs_send.at[r, c, k], rs_recv.at[r, c, k], {"sp": to * 2 + core}))
+            reduces.append(crossing)
+
         for c in range(chunks):
             if r == 0:
                 out_loads[c][0].wait()
@@ -172,18 +218,13 @@
             for n in range(peers):
                 block = share[n * rows : (n + 1) * rows, :]
                 whole[n, :, lanes] = block
-                part[r, n, :, lanes] = block.astype(BF16)
-            group = []
-            for k in range(1, peers):
-                to = lax.rem(me + k, peers)
-                copy = pltpu.make_async_remote_copy(
-                    src_ref=part.at[r, to, :, span], dst_ref=landed.at[r, k, :, span],
-                    send_sem=rs_send.at[r, c, k], recv_sem=rs_recv.at[r, c, k],
-                    device_id={"sp": to}, device_id_type=MESH)
-                copy.start()
-                group.append(copy)
-                sends.append(copy)
-            reduces.append(group)
+                part[r, n % 2, n // 2, :, lanes] = block.astype(BF16)
+            pairs.append(remote(
+                part.at[r, 1 - core, :, :, span], paired.at[r, :, :, span],
+                rs_send.at[r, c, 0], rs_recv.at[r, c, 0], {"sp": partner}))
+            if c > 0:
+                pass_on(c - 1)
+        pass_on(chunks - 1)
 
         shifts = []
         for c in range(chunks):
@@ -191,20 +232,15 @@
             span = pl.ds(c * cut, cut)
             for copy in reduces[c]:
                 copy.wait_recv()
-            summed = whole[me, :, lanes]
-            for k in range(1, peers):
+            summed = whole[me, :, lanes] + paired[r, group, :, lanes].astype(F32)
+            for k in range(1, groups):
                 summed = summed + landed[r, k, :, lanes].astype(F32)
             fresh[r, :, lanes] = (
                 gathered[r, me, :, lanes].astype(F32) + factors[2:3, lanes] * summed
             ).astype(BF16)
             target = gathered.at[r + 1, me, :, span] if r < ROUNDS - 1 else arrived.at[:, span]
-            copy = pltpu.make_async_remote_copy(
-                src_ref=fresh.at[r, :, span], dst_ref=target,
-                send_sem=sh_send.at[r, c], recv_sem=sh_recv.at[r, c],
-                device_id={"section": following}, device_id_type=MESH)
-            copy.start()
-            shifts.append(copy)
-            sends.append(copy)
+            shifts.append(remote(
+                fresh.at[r, :, span], target, sh_send.at[r, c], sh_recv.at[r, c], {"section": following}))
 
     for copy in shifts:
         copy.wait_recv()
@@ -230,11 +266,11 @@
     x, kv = pl.pallas_call(
         functools.partial(kernel, sections, peers),
         out_shape=(
-            jax.ShapeDtypeStruct((rows, width), BF16),
-            jax.ShapeDtypeStruct(kv_cache.shape[1:], BF16),
+            pltpu.VMEM((rows, width), BF16),
+            pltpu.VMEM(kv_cache.shape[1:], BF16),
         ),
         in_specs=[smem, smem, vmem, vmem, vmem] + [anywhere] * 5,
-        out_specs=(vmem, anywhere),
+        out_specs=(vmem, vmem),
         scratch_shapes=[
             pltpu.VMEM((3, width, local), BF16),
             pltpu.VMEM((width, hidden), BF16),
@@ -242,8 +278,10 @@
             pltpu.VMEM((hidden, width), BF16),
             pltpu.VMEM((2, tokens, local), BF16),
             pltpu.VMEM((ROUNDS, peers, rows, width), BF16),
-            pltpu.VMEM((ROUNDS, peers, rows, width), BF16),
-            pltpu.VMEM((ROUNDS, peers, rows, width), BF16),
+            pltpu.VMEM((ROUNDS, peers // 2, rows, width), BF16),
+            pltpu.VMEM((ROUNDS, peers // 2, rows, width), BF16),
+            pltpu.VMEM((ROUNDS, 2, peers // 2, rows, width), BF16),
+            pltpu.VMEM((ROUNDS, peers // 2, rows, width), BF16),
             pltpu.VMEM((peers, rows, width), F32),
             pltpu.VMEM((ROUNDS, rows, width), BF16),
             pltpu.VMEM((rows, width), BF16),

time: 54.3 us -> 52.8 us (0.972)
  local copies, waits for them, and re-layouts: 3.8 us -> 1.61 us
  Pallas kernels: 49.6 us -> 50.4 us
    unnamed x2, local copies, waits for them, and re-layouts: 3.8 us -> 1.61 us
    pallas_call x1, Pallas kernels: 49.6 us -> 50.4 us  [shards(): pl.pallas_call(functools.partial(kernel, sections, peers), out_shape=(plt...]
where the time goes in v2:
time: 52.8 us; the launch traced here: 52.6 us
  Pallas kernels  50.4 us (95%)
  local copies, waits for them, and re-layouts  1.61 us (3%)
  between operations  0.64 us (1%)
    pallas_call x1, Pallas kernels, shards(): pl.pallas_call(functools.partial(kernel, sections, peers), out_shape=(plt...  50.4 us
    unnamed x2, local copies, waits for them, and re-layouts  1.61 us

profile of v2, /device:TPU:0, one launch (start us, length us, event | category | flops | bytes accessed | tf_op | source)
XLA Modules:
  0.0 52.6 jit_solution(13442195789603888587)
XLA Ops:
  0.6 50.4 %shard_map.113 = (bf16[16,3072]{1,0:T(8,128)(2,1)S(1)}, bf16[2,512,512]{2,1,0:T(8,128)(2,1)S(1)}) custom-call(s32[8]{0:T(128)} %patch_ref.1, s32[8]{0:T(128)} %step_ref.1, bf16[16,3072]{1,0:T(8,128)(2,1)} %bitcast.22, bf16[3,28,3072]{2,1,0:T(8,128)(2,1)} %bitcast.21, bf16[2,128]{1,0:T(2,128)(2,1)} %bitcast.23, bf16[3,3072,512]{2,1,0:T(8,128)(2,1)} %bitcast.16, ...), custom_call_target="tpu_custom_call" | custom-call | tf_op jit(solution)/shard_map/pallas_call | solution.py:266
  51.0 0.6 %copy.14 = bf16[1,16,3072]{2,1,0:T(8,128)(2,1)} copy(bf16[1,16,3072]{2,1,0:T(8,128)(2,1)S(1)} %bitcast.15) | data formatting | bytes 196608
  51.6 1.0 %copy.15 = bf16[1,2,512,512]{3,2,1,0:T(8,128)(2,1)} copy(bf16[1,2,512,512]{3,2,1,0:T(8,128)(2,1)S(1)} %bitcast.14) | data formatting | bytes 2097152

commit v3 on v1

--- a/solution.py
+++ b/solution.py
@@ -61,9 +61,6 @@
     kv_load = pltpu.make_async_copy(kv_hbm, kv, kv_sem)
     for copy in qkv_loads:
         copy.start()
-    kv_load.start()
-    for copy in loads[3:]:
-        copy.start()
 
     barrier = pltpu.get_barrier_semaphore()
     for k in range(1, peers):
@@ -82,6 +79,9 @@
         copy.start()
         gathers[0].append(copy)
         sends.append(copy)
+    kv_load.start()
+    for copy in loads[3:]:
+        copy.start()
     gathered[0, me] = slots_ref[...]
 
     for r in range(ROUNDS):
@@ -230,11 +230,11 @@
     x, kv = pl.pallas_call(
         functools.partial(kernel, sections, peers),
         out_shape=(
-            jax.ShapeDtypeStruct((rows, width), BF16),
-            jax.ShapeDtypeStruct(kv_cache.shape[1:], BF16),
+            pltpu.VMEM((rows, width), BF16),
+            pltpu.VMEM(kv_cache.shape[1:], BF16),
         ),
         in_specs=[smem, smem, vmem, vmem, vmem] + [anywhere] * 5,
-        out_specs=(vmem, anywhere),
+        out_specs=(vmem, vmem),
         scratch_shapes=[
             pltpu.VMEM((3, width, local), BF16),
             pltpu.VMEM((width, hidden), BF16),

time: 54.3 us -> 52.3 us (0.963)
  local copies, waits for them, and re-layouts: 3.8 us -> 1.61 us
    unnamed x2, local copies, waits for them, and re-layouts: 3.8 us -> 1.61 us
where the time goes in v3:
time: 52.3 us; the launch traced here: 52.2 us
  Pallas kernels  49.9 us (95%)
  local copies, waits for them, and re-layouts  1.61 us (3%)
  between operations  0.64 us (1%)
    pallas_call x1, Pallas kernels, shards(): pl.pallas_call(functools.partial(kernel, sections, peers), out_shape=(plt...  49.9 us
    unnamed x2, local copies, waits for them, and re-layouts  1.61 us

profile of v3, /device:TPU:0, one launch (start us, length us, event | category | flops | bytes accessed | tf_op | source)
XLA Modules:
  0.0 52.2 jit_solution(8378500154784350445)
XLA Ops:
  0.6 49.9 %shard_map.113 = (bf16[16,3072]{1,0:T(8,128)(2,1)S(1)}, bf16[2,512,512]{2,1,0:T(8,128)(2,1)S(1)}) custom-call(s32[8]{0:T(128)} %patch_ref.1, s32[8]{0:T(128)} %step_ref.1, bf16[16,3072]{1,0:T(8,128)(2,1)} %bitcast.22, bf16[3,28,3072]{2,1,0:T(8,128)(2,1)} %bitcast.21, bf16[2,128]{1,0:T(2,128)(2,1)} %bitcast.23, bf16[3,3072,512]{2,1,0:T(8,128)(2,1)} %bitcast.16, ...), custom_call_target="tpu_custom_call" | custom-call | tf_op jit(solution)/shard_map/pallas_call | solution.py:230
  50.6 0.6 %copy.14 = bf16[1,16,3072]{2,1,0:T(8,128)(2,1)} copy(bf16[1,16,3072]{2,1,0:T(8,128)(2,1)S(1)} %bitcast.15) | data formatting | bytes 196608
  51.2 1.0 %copy.15 = bf16[1,2,512,512]{3,2,1,0:T(8,128)(2,1)} copy(bf16[1,2,512,512]{3,2,1,0:T(8,128)(2,1)S(1)} %bitcast.14) | data formatting | bytes 2097152
